TPU v7x, 512 devices: a whole 4x8x8 slice. The times are simulated.
512 devices in a mesh: mem: 64 (over z, x, core), bal: 8 (over y).
Axes of the slice: x: 4, y: 8, z: 8, core: 2. Of those that a mesh axis runs over, the one named last changes fastest.
Arguments:
- background_trials: bfloat16 [256, 1024, 256], P('mem', 'bal'), may hold values from -6 to 6
- mapped_readings: bfloat16 [256, 1024, 2048], P('mem', 'bal'), may hold values from -6 to 6
- measured_data: float32 [1024, 2048], P('bal'), may hold values from -9 to 9
- inverse_error_variance: float32 [1024, 2048], P('bal'), may hold values from 0.05 to 1
- measured_row_tally: int32 [1024], P('bal'), may hold values from 16 to 2032, as said below
Outputs:
- analysis: bfloat16 [256, 1024, 256], P('mem', 'bal')
Inputs may be any that keep to these rules, and one draw needn't show every extreme that they name: measured_row_tally[p] live rows, the first ones of patch p's block; in each aligned group of 2 consecutive patches the counts sum to at most 2048, and some group sums to exactly 2048.
All inputs are finite; a program needn't handle non-finite values.
Results may differ from a plain program's by a relative error of at most 0.0057.
Values may be sent and summed in bfloat16 or wider, within the bound.
No kernel may reach another device: no remote copies, remote signals or barrier semaphores. Data moves between devices by JAX's collectives and lax.ppermute only.
A program may use at most 64 MiB of HBM per device.

v0:
```python
import jax
import jax.numpy as jnp
from jax import lax
from jax.sharding import PartitionSpec as P

NS_ITERS = 7


def in_one_piece(arrays, axis, split_dim, concat_dim, along):
    both = jnp.concatenate(arrays, axis=along)
    out, at, done = (
        lax.all_to_all(both, axis, split_axis=split_dim, concat_axis=concat_dim, tiled=True),
        0,
        [],
    )
    for a in arrays:
        done.append(lax.slice_in_dim(out, at, at + a.shape[along], axis=along))
        at += a.shape[along]
    return tuple(done)


def prepare(ens, value, prec, count):
    rows = lax.iota(jnp.int32, ens.shape[1])
    mask = (rows < count).astype(jnp.float32)
    weight = mask * jnp.sqrt(prec)
    obs_mean = jnp.mean(ens, axis=0, dtype=jnp.float32)
    scaled = ((ens.astype(jnp.float32) - obs_mean) * weight).astype(jnp.bfloat16)
    misfit = weight * (value - obs_mean)
    vector = jnp.dot(scaled.astype(jnp.float32), misfit, precision=lax.Precision.HIGHEST)
    return (scaled, vector)


def complete_step(gram, vector, region_variables):
    members = gram.shape[0]
    identity = jnp.eye(members, dtype=jnp.float32)
    amat = gram + (members - 1.0) * identity
    frobenius = jnp.sqrt(jnp.sum(amat * amat))
    iterate = amat / frobenius
    inverse = identity
    for step in range(NS_ITERS):
        middle = 1.5 * identity - 0.5 * jnp.dot(inverse, iterate, precision=lax.Precision.HIGHEST)
        iterate = jnp.dot(iterate, middle, precision=lax.Precision.HIGHEST)
        inverse = jnp.dot(middle, inverse, precision=lax.Precision.HIGHEST)
    spread = jnp.sqrt((members - 1.0) / frobenius) * inverse
    inner = jnp.dot(inverse, vector, precision=lax.Precision.HIGHEST)
    mean_weights = jnp.dot(inverse, inner, precision=lax.Precision.HIGHEST) / frobenius
    transform = (spread + mean_weights[:, None]).astype(jnp.bfloat16)
    state_mean = jnp.mean(region_variables, axis=0, dtype=jnp.float32)
    perturb = (region_variables.astype(jnp.float32) - state_mean).astype(jnp.bfloat16)
    moved = jnp.dot(transform.T, perturb, preferred_element_type=jnp.float32)
    return (state_mean + moved).astype(jnp.bfloat16)


def on_device(
    background_trials, mapped_readings, measured_data, inverse_error_variance, measured_row_tally
):
    partner_processors = lax.axis_size("mem")
    region_batch = background_trials.shape[1] // partner_processors
    offset = lax.axis_index("mem") * region_batch
    value = lax.dynamic_slice_in_dim(measured_data, offset, region_batch, 0)
    prec = lax.dynamic_slice_in_dim(inverse_error_variance, offset, region_batch, 0)
    count = lax.dynamic_slice_in_dim(measured_row_tally, offset, region_batch, 0)
    region_variables, ens = in_one_piece((background_trials, mapped_readings), "mem", 1, 0, 2)
    scaled, vector = jax.vmap(prepare, in_axes=(1, 0, 0, 0))(ens, value, prec, count)
    gram = jnp.einsum("pkr,plr->pkl", scaled, scaled, preferred_element_type=jnp.float32)
    corrected_trials = jax.vmap(complete_step, in_axes=(0, 0, 1), out_axes=1)(
        gram, vector, region_variables
    )
    return lax.all_to_all(corrected_trials, "mem", split_axis=0, concat_axis=1, tiled=True)


def solution(mesh):
    return jax.shard_map(
        on_device,
        mesh=mesh,
        in_specs=(
            P("mem", "bal", None),
            P("mem", "bal", None),
            P("bal", None),
            P("bal", None),
            P("bal"),
        ),
        out_specs=P("mem", "bal", None),
        check_vma=False,
    )
```

profile of v0, /device:TPU:1, one launch (start us, length us, event | category | flops | bytes accessed | tf_op | source)
XLA Modules:
  0.0 122.8 jit_solution(5436246117650324126)
XLA Ops:
  0.0 0.0 copy-start
  0.0 3.3 %copy.10 = bf16[4,128,2048]{2,0,1:T(4,128)(2,1)S(1)} copy(bf16[4,128,2048]{2,1,0:T(8,128)(2,1)} %param.6) | data formatting | bytes 4194304 | tf_op args[1]
  3.3 0.0 copy-done
  3.3 0.2 copy.9
  3.5 2.6 %pad_maximum_fusion = bf16[4,128,2304]{2,0,1:T(4,128)(2,1)} fusion(bf16[4,128,2048]{2,0,1:T(4,128)(2,1)S(1)} %copy.10, bf16[4,128,256]{2,0,1:T(4,128)(2,1)S(1)} %copy.9), kind=kLoop, calls=%fused_computation.4 | loop fusion | flops 4718592 | bytes 4718592 | tf_op jit(solution)/shard_map/concatenate | solution.py:10
  6.1 0.0 copy-start.1
  6.1 15.0 %all-to-all-start = ((bf16[4,128,2304]{2,0,1:T(4,128)(2,1)}), bf16[4,128,2304]{2,0,1:T(4,128)(2,1)S(1)}, u32[]{:S(2)}, u32[]{:S(2)}) async-start(bf16[4,128,2304]{2,0,1:T(4,128)(2,1)} %pad_maximum_fusion), calls=%async_computation | async-start | bytes 4718592 | tf_op jit(solution)/shard_map/all_to_all | solution.py:12
  21.0 0.0 copy-done.1
  21.0 0.1 dynamic_slice.9
  21.2 55.2 %all-to-all-done = bf16[4,128,2304]{2,0,1:T(4,128)(2,1)S(1)} async-done(((bf16[4,128,2304]{2,0,1:T(4,128)(2,1)}), bf16[4,128,2304]{2,0,1:T(4,128)(2,1)S(1)}, u32[]{:S(2)}, u32[]{:S(2)}) %all-to-all-start) | async-done | bytes 2359328 | tf_op jit(solution)/shard_map/all_to_all | solution.py:12
  76.4 2.2 %copy.11 = bf16[64,4,2,2304]{3,1,0,2:T(4,128)(2,1)} copy(bf16[64,4,2,2304]{3,1,2,0:T(4,128)(2,1)S(1)} %bitcast.77) | data formatting | bytes 4718592 | tf_op jit(solution)/shard_map/all_to_all | solution.py:12
  78.6 4.0 %all_to_all.29 = bf16[256,2,2304]{2,0,1:T(8,128)(2,1)S(1)} reshape(bf16[64,4,2,2304]{3,1,0,2:T(4,128)(2,1)} %copy.11) | data formatting | bytes 4718592 | tf_op jit(solution)/shard_map/all_to_all | solution.py:12
  82.6 0.3 convert_reduce_fusion
  83.0 1.0 multiply_bitcast_fusion
  83.9 1.2 multiply_reduce_fusion
  85.1 0.5 fusion.14
  85.7 0.7 fusion.33
  86.4 0.4 fusion.29
  86.8 0.7 fusion.12
  87.5 0.7 fusion.40
  88.1 0.7 fusion.39
  88.8 0.7 fusion.11
  89.5 0.7 fusion.42
  90.1 0.7 fusion.41
  90.8 0.7 fusion.10
  91.5 0.7 fusion.44
  92.1 0.7 fusion.43
  92.8 0.7 fusion.9
  93.5 0.7 fusion.46
  94.1 0.7 fusion.45
  94.8 0.7 fusion.8
  95.5 0.9 fusion.48
  96.4 0.7 fusion.47
  97.0 0.1 convert_reduce_fusion.1
  97.1 0.7 fusion.7
  97.8 0.7 fusion.49
  98.4 1.7 %fusion.3 = f32[2,1,256]{2,1,0:T(1,128)S(1)} fusion(f32[2,2048]{1,0:T(2,128)S(1)} %get-tuple-element.6, f32[2,2048]{1,0:T(2,128)S(1)} %get-tuple-element.7, bf16[256,2,2304]{2,0,1:T(8,128)(2,1)S(1)} %all_to_all.29, f32[2,2048,1]{1,0,2:T(2,128)S(1)} %get-tuple-element.5), kind=kOutput, calls=%fused_computation.6 | convolution fusion | flops 16777216 | bytes 2148352 | tf_op jit(solution)/shard_map/vmap()/dot_general | solution.py:29
  100.2 0.6 fusion.37
  100.7 0.6 fusion.35
  101.3 0.1 bitcast_divide_fusion
  101.3 0.4 fusion.19
  101.8 0.3 copy.13
  102.0 19.8 %all_to_all.36 = bf16[256,2,256]{2,1,0:T(2,128)(2,1)S(1)} all-to-all(bf16[256,2,256]{2,1,0:T(2,128)(2,1)S(1)} %copy.13), channel_id=1, replica_groups=mesh['mem'=64,'bal'=8] {'mem'}, dimensions={0} | all-to-all | bytes 524288 | tf_op jit(solution)/shard_map/all_to_all | solution.py:69
  121.8 0.2 copy.14
  122.0 0.8 all_to_all.33
  (5 shorter events, 0.1 us)
Async XLA Ops:
  0.0 3.3 %copy-start = (bf16[4,128,256]{2,1,0:T(8,128)(2,1)S(1)}, bf16[4,128,256]{2,1,0:T(8,128)(2,1)}, u32[]{:S(2)}) copy-start(bf16[4,128,256]{2,1,0:T(8,128)(2,1)} %param.5) | copy-start | bytes 786436
  6.1 15.0 %copy-start.1 = (s32[128]{0:T(128)S(1)}, s32[128]{0:T(128)}, u32[]{:S(2)}) copy-start(s32[128]{0:T(128)} %param.9) | copy-start | bytes 1540
  6.1 70.3 %all-to-all-start = ((bf16[4,128,2304]{2,0,1:T(4,128)(2,1)}), bf16[4,128,2304]{2,0,1:T(4,128)(2,1)S(1)}, u32[]{:S(2)}, u32[]{:S(2)}) async-start(bf16[4,128,2304]{2,0,1:T(4,128)(2,1)} %pad_maximum_fusion), calls=%async_computation | async-start | bytes 4718592 | tf_op jit(solution)/shard_map/all_to_all | solution.py:12
where the time goes:
time: 123 us
  waiting for transfers between devices  55.2 us (45%)
  blocking collectives  19.8 us (16%)
  matrix products  17.5 us (14%)
  starting transfers between devices  15 us (12%)
  local copies, waits for them, and re-layouts  11 us (9%)
  other arithmetic  4.06 us (3%)
    all_to_all x1, waiting for transfers between devices, in_one_piece(): lax.all_to_all(both, axis, split_axis=split_dim, concat_axis=concat_dim,...  55.2 us
    all_to_all x1, blocking collectives, on_device(): lax.all_to_all(corrected_trials, 'mem', split_axis=0, concat_axis=1, tile...  19.8 us
    all_to_all x1, starting transfers between devices, in_one_piece(): lax.all_to_all(both, axis, split_axis=split_dim, concat_axis=concat_dim,...  15 us
    all_to_all x2, local copies, waits for them, and re-layouts, in_one_piece(): lax.all_to_all(both, axis, split_axis=split_dim, concat_axis=concat_dim,...  6.23 us
    dot_general x7, matrix products, complete_step(): jnp.dot(inverse, iterate, precision=lax.Precision.HIGHEST)  4.52 us
    dot_general x7, matrix products, complete_step(): inverse = jnp.dot(middle, inverse, precision=lax.Precision.HIGHEST)  4.34 us
    dot_general x6, matrix products, complete_step(): iterate = jnp.dot(iterate, middle, precision=lax.Precision.HIGHEST)  4.2 us
    unnamed x6, local copies, waits for them, and re-layouts  3.47 us
  transfers between devices with their start and end apart: 1, of which 1 were waited for; matrix products, arithmetic and copies ran while one was open for 0% of the time, Pallas kernels for 0%

commit v1 on v0

v1 whole, which is shorter than its diff:
```python
import functools

import jax
import jax.numpy as jnp
from jax import lax
from jax.experimental import pallas as pl
from jax.experimental.pallas import tpu as pltpu
from jax.sharding import PartitionSpec as P

NS_ITERS = 7
F32 = jnp.float32
BF16 = jnp.bfloat16
PACK_VMEM = 56 * 1024 * 1024
ANALYSE_VMEM = 20 * 1024 * 1024


def iotas(rows, columns):
    return (
        lax.broadcasted_iota(jnp.int32, (rows, columns), 0),
        lax.broadcasted_iota(jnp.int32, (rows, columns), 1),
    )


def one_hot(test):
    return jnp.where(test, 1.0, 0.0).astype(BF16)


def mm(a, b):
    return jnp.dot(a, b, preferred_element_type=F32)


def mm_nt(a, b):
    return lax.dot_general(a, b, (((1,), (1,)), ((), ())), preferred_element_type=F32)


def flip(size):
    r, c = iotas(size, size)
    return one_hot(r + c == size - 1)


def pack_kernel(tally_ref, ens_ref, state_ref, packed_ref):
    pairs = packed_ref.shape[0] // 8
    patches = 2 * pairs
    half = ens_ref.shape[2] // 2
    block = pl.program_id(0)
    rows = 8 * pairs
    r, k = iotas(rows, 2 * rows)
    pair, top, member = r >> 3, (r >> 2) & 1, r & 3
    take_a = one_hot(k == top * rows + member * patches + 2 * pair)
    take_b = one_hot(k == (1 - top) * rows + member * patches + 2 * pair + 1)
    x = jnp.concatenate(
        [
            ens_ref[:, :, :half].reshape(rows, half),
            ens_ref[:, :, half:].reshape(rows, half),
        ],
        axis=0,
    )
    first = mm(take_a, x)
    second = mm(take_b, x).astype(BF16)
    r1, l1 = iotas(rows, tally_ref.shape[1])
    wanted = l1 == 2 * (block * pairs + (r1 >> 3))
    limit = jnp.sum(jnp.where(wanted, tally_ref[...].astype(F32), 0.0), axis=1, keepdims=True)
    limit = limit - jnp.where((r1[:, :1] >> 2) & 1 == 1, float(half), 0.0)
    turn = flip(256)
    parts = half // 256
    for q in range(parts):
        lanes = slice(q * 256, (q + 1) * 256)
        back = slice((parts - 1 - q) * 256, (parts - q) * 256)
        _, slot = iotas(rows, 256)
        slot = (slot + q * 256).astype(F32)
        packed_ref[:, lanes] = jnp.where(
            slot < limit, first[:, lanes], mm(second[:, back], turn)
        ).astype(BF16)
    r2, k2 = iotas(rows, rows)
    take_s = one_hot(k2 == (r2 & 3) * patches + (r2 >> 2))
    packed_ref[:, half:] = mm(take_s, state_ref[...].reshape(rows, state_ref.shape[2])).astype(BF16)


def pack(tally, ens, state, interpret=False):
    members, patches, slots = ens.shape
    width = state.shape[2]
    steps = 2
    per = patches // steps
    rows = 4 * patches
    return pl.pallas_call(
        pack_kernel,
        grid=(steps,),
        in_specs=[
            pl.BlockSpec((1, patches), lambda i: (0, 0)),
            pl.BlockSpec((members, per, slots), lambda i: (0, i, 0)),
            pl.BlockSpec((members, per, width), lambda i: (0, i, 0)),
        ],
        out_specs=pl.BlockSpec((rows // steps, slots // 2 + width), lambda i: (i, 0)),
        out_shape=jax.ShapeDtypeStruct((rows, slots // 2 + width), BF16),
        compiler_params=pltpu.CompilerParams(vmem_limit_bytes=PACK_VMEM),
        cost_estimate=pl.CostEstimate(
            flops=10**9, bytes_accessed=5 * 2**20, transcendentals=0
        ),
        interpret=interpret,
    )(tally.reshape(1, patches), ens, state)


def weights_kernel(me_ref, tally_ref, value_ref, prec_ref, out_ref):
    slots = value_ref.shape[1]
    row = 2 * (me_ref[0] % 4)
    count_a = tally_ref[2 * me_ref[0]]
    count_b = tally_ref[2 * me_ref[0] + 1]
    parts = slots // 256
    value = value_ref[...]
    prec = prec_ref[...]
    which, slot = iotas(8, slots)

    def pick(x, i):
        return jnp.sum(jnp.where(which == row + i, x, 0.0), axis=0, keepdims=True)

    value_b = pick(value, 1)
    prec_b = pick(prec, 1)
    cut = [b[:, i * 256 : (i + 1) * 256] for b in (value_b, prec_b) for i in range(parts)]
    r, c = iotas(256, 256)
    turn = jnp.where(r + c == 255, 1.0, 0.0)
    turned = jnp.dot(
        jnp.concatenate(cut, axis=0),
        turn,
        precision=lax.Precision.HIGHEST,
        preferred_element_type=F32,
    )
    back = [
        jnp.concatenate(
            [turned[j * parts + i : j * parts + i + 1] for i in reversed(range(parts))], axis=1
        )
        for j in range(2)
    ]
    slot = slot[:1]
    is_a = slot < count_a
    is_b = slot >= slots - count_b
    weight_a = jnp.where(is_a, jnp.sqrt(pick(prec, 0)), 0.0)
    weight_b = jnp.where(is_b & ~is_a, jnp.sqrt(back[1]), 0.0)
    seen = jnp.where(is_a, pick(value, 0), back[0])
    out_ref[0:1, :] = weight_a
    out_ref[1:2, :] = weight_b
    out_ref[2:3, :] = seen
    out_ref[3:8, :] = jnp.zeros((5, slots), F32)


def pair_weights(me, tally, value, prec, interpret=False):
    slots = value.shape[1]
    return pl.pallas_call(
        weights_kernel,
        grid_spec=pltpu.PrefetchScalarGridSpec(
            num_scalar_prefetch=2,
            grid=(1,),
            in_specs=[pl.BlockSpec((8, slots), lambda i, me, t: (me[0] // 4, 0))] * 2,
            out_specs=pl.BlockSpec((8, slots), lambda i, me, t: (0, 0)),
        ),
        out_shape=jax.ShapeDtypeStruct((8, slots), F32),
        compiler_params=pltpu.CompilerParams(vmem_limit_bytes=16 * 1024 * 1024),
        interpret=interpret,
    )(me, tally, value, prec)


def split(x):
    hi = x.astype(BF16)
    return hi, (x - hi.astype(F32)).astype(BF16)


def mm3(a, b):
    ah, al = a
    bh, bl = b
    return mm(
        jnp.concatenate([ah, ah, al], axis=1), jnp.concatenate([bh, bl, bh], axis=0)
    )


def newton_schulz(ts, eye):
    zs = [1.5 * eye - 0.5 * t for t in ts]
    for step in range(1, NS_ITERS):
        cut = [split(t) for t in ts]
        squares = [mm3(c, c) for c in cut]
        cubes = [mm3(c, split(q)) for c, q in zip(cut, squares)]
        ts = [2.25 * t - 1.5 * q + 0.25 * u for t, q, u in zip(ts, squares, cubes)]
        if step < 4:
            zs = [1.5 * z - 0.5 * mm3(split(t), split(z)) for t, z in zip(ts, zs)]
        else:
            zs = [z + 0.5 * mm3(split(eye - t), split(z)) for t, z in zip(ts, zs)]
    return zs


def centring_matrix(part):
    r, k = iotas(264, 512)
    ours = (k >> 2) & 1 == part
    own = k == (r >> 2) * 8 + part * 4 + (r & 3)
    share = jnp.where(r < 256, -1.0 / 256.0, 1.0 / 256.0)
    return (jnp.where(ours, share, 0.0) + jnp.where(own & (r < 256), 1.0, 0.0)).astype(BF16)


def analysis_kernel(recv_ref, rows_ref, out_ref, s_ref, all_ref, perturb_ref):
    slots = rows_ref.shape[1]
    half = slots // 2
    means, middles = [], []
    for part in range(2):
        centre = centring_matrix(part)
        for q in range(half // 256):
            at = slice(part * half + q * 256, part * half + (q + 1) * 256)
            apart = mm(centre, recv_ref[:, q * 256 : (q + 1) * 256])
            means.append(apart[256:257])
            apart = apart[:256]
            weight_a, weight_b = rows_ref[0:1, at], rows_ref[1:2, at]
            s_ref[0:256, at] = (apart * weight_a).astype(BF16)
            s_ref[256:512, at] = (apart * weight_b).astype(BF16)
            all_ref[:, at] = (apart * (weight_a + weight_b)).astype(BF16)
        apart = mm(centre, recv_ref[:, half:])
        middles.append(apart[256:257])
        perturb_ref[part] = apart[:256].astype(BF16)
    mean = jnp.concatenate(means, axis=1)
    weight_a, weight_b, seen = rows_ref[0:1, :], rows_ref[1:2, :], rows_ref[2:3, :]
    rest = []
    for w in (weight_a, weight_b):
        left = w * (seen - mean)
        for _ in range(3):
            top = left.astype(BF16).astype(F32)
            rest.append(top)
            left = left - top
    rest += [jnp.zeros_like(mean)] * 10
    s_ref[512:528, :] = jnp.concatenate(rest, axis=0).astype(BF16)
    both = mm_nt(s_ref[...], all_ref[...])
    r, c = iotas(256, 256)
    eye = jnp.where(r == c, 1.0, 0.0)
    amat = [both[256 * p : 256 * (p + 1)] + 255.0 * eye for p in range(2)]
    fro = [jnp.sqrt(jnp.sum(a * a)) for a in amat]
    z = newton_schulz([a * (1.0 / f) for a, f in zip(amat, fro)], eye)
    done = []
    for p in range(2):
        v = jnp.sum(both[512 + 3 * p : 515 + 3 * p], axis=0, keepdims=True)
        inner = jnp.sum(z[p] * v, axis=1, keepdims=True)
        mean_weights = jnp.sum(z[p] * inner, axis=0, keepdims=True) / fro[p]
        transform = (jnp.sqrt(255.0 / fro[p]) * z[p] + mean_weights).astype(BF16)
        done.append((middles[p] + mm(transform, perturb_ref[p])).astype(BF16))
    k, r = iotas(256, 256)
    scatter = one_hot(k == ((r & 127) >> 2) * 8 + (r >> 7) * 4 + (r & 3))
    for g in range(2):
        pair = jnp.concatenate([d[128 * g : 128 * (g + 1)] for d in done], axis=0)
        out_ref[256 * g : 256 * (g + 1), :] = mm(scatter, pair).astype(BF16)


def analyse(recv, rows, interpret=False):
    total, wide = recv.shape
    slots = rows.shape[1]
    width = wide - slots // 2
    return pl.pallas_call(
        analysis_kernel,
        out_shape=jax.ShapeDtypeStruct((total, width), BF16),
        scratch_shapes=[
            pltpu.VMEM((528, slots), BF16),
            pltpu.VMEM((256, slots), BF16),
            pltpu.VMEM((2, 256, width), BF16),
        ],
        compiler_params=pltpu.CompilerParams(vmem_limit_bytes=ANALYSE_VMEM),
        cost_estimate=pl.CostEstimate(
            flops=5 * 10**9, bytes_accessed=2 * 2**20, transcendentals=0
        ),
        interpret=interpret,
    )(recv, rows)


def unpack_kernel(recv_ref, out_ref):
    r, k = iotas(256, 256)
    gather = one_hot(k == (r & 63) * 4 + (r >> 6))
    for g in range(2):
        moved = mm(gather, recv_ref[256 * g : 256 * (g + 1), :]).astype(BF16)
        out_ref[:, 64 * g : 64 * (g + 1), :] = moved.reshape(4, 64, recv_ref.shape[1])


def unpack(recv, interpret=False):
    rows, width = recv.shape
    return pl.pallas_call(
        unpack_kernel,
        out_shape=jax.ShapeDtypeStruct((4, rows // 4, width), BF16),
        compiler_params=pltpu.CompilerParams(vmem_limit_bytes=16 * 1024 * 1024),
        interpret=interpret,
    )(recv)


def exchange(x):
    return lax.all_to_all(x, "mem", split_axis=0, concat_axis=0, tiled=True)


def on_device(
    background_trials, mapped_readings, measured_data, inverse_error_variance, measured_row_tally
):
    me = lax.axis_index("mem").astype(jnp.int32).reshape(1)
    packed = pack(measured_row_tally, mapped_readings, background_trials)
    received = exchange(packed)
    rows = pair_weights(me, measured_row_tally, measured_data, inverse_error_variance)
    return unpack(exchange(analyse(received, rows)))


def solution(mesh):
    return jax.shard_map(
        on_device,
        mesh=mesh,
        in_specs=(
            P("mem", "bal", None),
            P("mem", "bal", None),
            P("bal", None),
            P("bal", None),
            P("bal"),
        ),
        out_specs=P("mem", "bal", None),
        check_vma=False,
    )
```

time: 123 us -> 81.2 us (0.66)
  waiting for transfers between devices: 55.2 us -> 32.8 us
  matrix products: 17.5 us -> 0 us
  Pallas kernels: 0 us -> 14 us
  local copies, waits for them, and re-layouts: 11 us -> 0.01 us
  other arithmetic: 4.06 us -> 0 us
    all_to_all x1, waiting for transfers between devices: 55.2 us -> 32.8 us  [exchange(): return lax.all_to_all(x, 'mem', split_axis=0, concat_axis=0, tiled=True)]
    dot_general x25 -> x0, matrix products: 17.5 us -> none  [the longest x7 4.52 us: complete_step(): jnp.dot(inverse, iterate, precision=lax.Precision.HIGHEST)]
    pallas_call x0 -> x4, Pallas kernels: none -> 14 us  [the longest x1 8.1 us: analyse(): pl.pallas_call(analysis_kernel, out_shape=jax.ShapeDtypeStruct((total, wi...]
    all_to_all x4 -> x0, local copies, waits for them, and re-layouts: 7.22 us -> none  [the longest x2 6.23 us: in_one_piece(): lax.all_to_all(both, axis, split_axis=split_dim, concat_axis=concat_dim,...]
    unnamed x6, local copies, waits for them, and re-layouts: 3.47 us -> 0.01 us
    concatenate x1 -> x0, other arithmetic: 2.58 us -> none  [in_one_piece(): both = jnp.concatenate(arrays, axis=along)]
  transfers between devices with their start and end apart: 1 -> 1, of which waited for: 1 -> 1; matrix products, arithmetic and copies ran while one was open for 0% -> 0% of each run, Pallas kernels for 0% -> 1%
where the time goes in v1:
time: 81.2 us; the launch traced here: 81 us
  waiting for transfers between devices  32.8 us (40%)
  blocking collectives  19.2 us (24%)
  starting transfers between devices  15 us (18%)
  Pallas kernels  14 us (17%)
    all_to_all x1, waiting for transfers between devices, exchange(): return lax.all_to_all(x, 'mem', split_axis=0, concat_axis=0, tiled=True)  32.8 us
    all_to_all x1, blocking collectives, exchange(): return lax.all_to_all(x, 'mem', split_axis=0, concat_axis=0, tiled=True)  19.2 us
    all_to_all x1, starting transfers between devices, exchange(): return lax.all_to_all(x, 'mem', split_axis=0, concat_axis=0, tiled=True)  15 us
    pallas_call x1, Pallas kernels, analyse(): pl.pallas_call(analysis_kernel, out_shape=jax.ShapeDtypeStruct((total, wi...  8.1 us
    pallas_call x1, Pallas kernels, pack(): pl.pallas_call(pack_kernel, grid=(steps,), in_specs=[pl.BlockSpec((1, pat...  4.14 us
  transfers between devices with their start and end apart: 1, of which 1 were waited for; matrix products, arithmetic and copies ran while one was open for 0% of the time, Pallas kernels for 1%

profile of v1, /device:TPU:1, one launch (start us, length us, event | category | flops | bytes accessed | tf_op | source)
XLA Modules:
  0.0 81.0 jit_solution(8680179474095999684)
XLA Ops:
  0.0 4.1 %shard_map.55 = bf16[512,1280]{1,0:T(8,128)(2,1)} custom-call(s32[1,128]{1,0:T(1,128)} %bitcast.9, bf16[4,128,2048]{2,1,0:T(8,128)(2,1)} %ens_ref.1, bf16[4,128,256]{2,1,0:T(8,128)(2,1)} %state_ref.1), custom_call_target="tpu_custom_call" | custom-call | flops 1000000000 | bytes 5242880 | tf_op jit(solution)/shard_map/pallas_call | solution.py:85
  4.1 0.0 copy-start
  4.1 0.0 copy-start.1
  4.1 0.0 copy-start.2
  4.2 15.0 %all-to-all-start = ((bf16[64,8,1280]{2,1,0:T(8,128)(2,1)}), bf16[64,8,1280]{2,1,0:T(8,128)(2,1)S(1)}, u32[]{:S(2)}, u32[]{:S(2)}) async-start(bf16[64,8,1280]{2,1,0:T(8,128)(2,1)} %bitcast.10), calls=%async_computation | async-start | bytes 2621440 | tf_op jit(solution)/shard_map/all_to_all | solution.py:284
  19.1 0.0 copy-done
  19.1 0.0 copy-done.1
  19.2 0.0 copy-done.2
  19.2 0.8 %shard_map.56.rows_ref = f32[8,2048]{1,0:T(8,128)S(1)} custom-call(s32[1]{0:T(128)} %bitcast.3.me_ref, s32[128]{0:T(128)S(1)} %copy-done.2, f32[128,2048]{1,0:T(8,128)S(1)} %copy-done, f32[128,2048]{1,0:T(8,128)S(1)} %copy-done.1), custom_call_target="tpu_custom_call" | custom-call | tf_op jit(solution)/shard_map/pallas_call | solution.py:147
  20.0 32.8 %all-to-all-done = bf16[64,8,1280]{2,1,0:T(8,128)(2,1)S(1)} async-done(((bf16[64,8,1280]{2,1,0:T(8,128)(2,1)}), bf16[64,8,1280]{2,1,0:T(8,128)(2,1)S(1)}, u32[]{:S(2)}, u32[]{:S(2)}) %all-to-all-start) | async-done | bytes 1310752 | tf_op jit(solution)/shard_map/all_to_all | solution.py:284
  52.8 8.1 %shard_map.57 = bf16[512,256]{1,0:T(8,128)(2,1)S(1)} custom-call(bf16[512,1280]{1,0:T(8,128)(2,1)S(1)} %bitcast.6, f32[8,2048]{1,0:T(8,128)S(1)} %shard_map.56.rows_ref), custom_call_target="tpu_custom_call" | custom-call | flops 5000000000 | bytes 2097152 | tf_op jit(solution)/shard_map/pallas_call | solution.py:249
  60.9 19.2 %all_to_all.22 = bf16[64,8,256]{2,1,0:T(8,128)(2,1)S(1)} all-to-all(bf16[64,8,256]{2,1,0:T(8,128)(2,1)S(1)} %bitcast.8), channel_id=1, replica_groups=mesh['mem'=64,'bal'=8] {'mem'}, dimensions={0} | all-to-all | bytes 524288 | tf_op jit(solution)/shard_map/all_to_all | solution.py:284
  80.1 0.9 %shard_map.58 = bf16[4,128,256]{2,1,0:T(8,128)(2,1)} custom-call(bf16[512,256]{1,0:T(8,128)(2,1)S(1)} %bitcast.7), custom_call_target="tpu_custom_call" | custom-call | tf_op jit(solution)/shard_map/pallas_call | solution.py:275
Async XLA Ops:
  4.1 15.0 %copy-start = (f32[128,2048]{1,0:T(8,128)S(1)}, f32[128,2048]{1,0:T(8,128)}, u32[]{:S(2)}) copy-start(f32[128,2048]{1,0:T(8,128)} %value_ref.1) | copy-start | bytes 3145732
  4.1 15.0 %copy-start.1 = (f32[128,2048]{1,0:T(8,128)S(1)}, f32[128,2048]{1,0:T(8,128)}, u32[]{:S(2)}) copy-start(f32[128,2048]{1,0:T(8,128)} %prec_ref.1) | copy-start | bytes 3145732
  4.1 15.0 %copy-start.2 = (s32[128]{0:T(128)S(1)}, s32[128]{0:T(128)}, u32[]{:S(2)}) copy-start(s32[128]{0:T(128)} %tally_ref.1) | copy-start | bytes 1540
  4.2 48.6 %all-to-all-start = ((bf16[64,8,1280]{2,1,0:T(8,128)(2,1)}), bf16[64,8,1280]{2,1,0:T(8,128)(2,1)S(1)}, u32[]{:S(2)}, u32[]{:S(2)}) async-start(bf16[64,8,1280]{2,1,0:T(8,128)(2,1)} %bitcast.10), calls=%async_computation | async-start | bytes 2621440 | tf_op jit(solution)/shard_map/all_to_all | solution.py:284

commit v2 on v1

--- a/solution.py
+++ b/solution.py
@@ -38,42 +38,50 @@
     return one_hot(r + c == size - 1)
 
 
-def pack_kernel(tally_ref, ens_ref, state_ref, packed_ref):
-    pairs = packed_ref.shape[0] // 8
+def pack_kernel(tally_ref, ens_ref, state_ref, packed_ref, second_ref):
+    pairs = 16
     patches = 2 * pairs
+    rows = 8 * pairs
     half = ens_ref.shape[2] // 2
-    block = pl.program_id(0)
-    rows = 8 * pairs
-    r, k = iotas(rows, 2 * rows)
-    pair, top, member = r >> 3, (r >> 2) & 1, r & 3
-    take_a = one_hot(k == top * rows + member * patches + 2 * pair)
-    take_b = one_hot(k == (1 - top) * rows + member * patches + 2 * pair + 1)
-    x = jnp.concatenate(
-        [
-            ens_ref[:, :, :half].reshape(rows, half),
-            ens_ref[:, :, half:].reshape(rows, half),
-        ],
-        axis=0,
-    )
-    first = mm(take_a, x)
-    second = mm(take_b, x).astype(BF16)
-    r1, l1 = iotas(rows, tally_ref.shape[1])
-    wanted = l1 == 2 * (block * pairs + (r1 >> 3))
-    limit = jnp.sum(jnp.where(wanted, tally_ref[...].astype(F32), 0.0), axis=1, keepdims=True)
-    limit = limit - jnp.where((r1[:, :1] >> 2) & 1 == 1, float(half), 0.0)
-    turn = flip(256)
     parts = half // 256
-    for q in range(parts):
-        lanes = slice(q * 256, (q + 1) * 256)
-        back = slice((parts - 1 - q) * 256, (parts - q) * 256)
-        _, slot = iotas(rows, 256)
-        slot = (slot + q * 256).astype(F32)
-        packed_ref[:, lanes] = jnp.where(
-            slot < limit, first[:, lanes], mm(second[:, back], turn)
-        ).astype(BF16)
+    groups = packed_ref.shape[0] // rows
+    r, k = iotas(2 * rows, 2 * rows)
+    local = r & (rows - 1)
+    last = r // rows
+    top = (((local >> 2) & 1) ^ last) * rows
+    take = one_hot(k == top + (local & 3) * patches + 2 * (local >> 3) + last)
     r2, k2 = iotas(rows, rows)
     take_s = one_hot(k2 == (r2 & 3) * patches + (r2 >> 2))
-    packed_ref[:, half:] = mm(take_s, state_ref[...].reshape(rows, state_ref.shape[2])).astype(BF16)
+    turn = flip(256)
+    r1, l1 = iotas(rows, tally_ref.shape[1])
+    tally = tally_ref[...].astype(F32)
+    lower = jnp.where((r1[:, :1] >> 2) & 1 == 1, float(half), 0.0)
+    _, lane = iotas(rows, 256)
+    lane = lane.astype(F32)
+    for g in range(groups):
+        own = slice(g * patches, (g + 1) * patches)
+        there = slice(g * rows, (g + 1) * rows)
+        wanted = l1 == 2 * ((pl.program_id(0) * groups + g) * pairs + (r1 >> 3))
+        limit = jnp.sum(jnp.where(wanted, tally, 0.0), axis=1, keepdims=True) - lower
+        first = []
+        for q in range(parts):
+            lanes = slice(q * 256, (q + 1) * 256)
+            far = slice(half + q * 256, half + (q + 1) * 256)
+            x = jnp.concatenate(
+                [ens_ref[:, own, lanes].reshape(rows, 256), ens_ref[:, own, far].reshape(rows, 256)],
+                axis=0,
+            )
+            both = mm(take, x)
+            first.append(both[:rows])
+            second_ref[(parts - 1 - q) * rows : (parts - q) * rows, :] = both[rows:].astype(BF16)
+        turned = mm(second_ref[...], turn)
+        for q in range(parts):
+            packed_ref[there, q * 256 : (q + 1) * 256] = jnp.where(
+                lane < limit - q * 256.0, first[q], turned[q * rows : (q + 1) * rows]
+            ).astype(BF16)
+        packed_ref[there, half:] = mm(
+            take_s, state_ref[:, own, :].reshape(rows, state_ref.shape[2])
+        ).astype(BF16)
 
 
 def pack(tally, ens, state, interpret=False):
@@ -92,6 +100,7 @@
         ],
         out_specs=pl.BlockSpec((rows // steps, slots // 2 + width), lambda i: (i, 0)),
         out_shape=jax.ShapeDtypeStruct((rows, slots // 2 + width), BF16),
+        scratch_shapes=[pltpu.VMEM((512, 256), BF16)],
         compiler_params=pltpu.CompilerParams(vmem_limit_bytes=PACK_VMEM),
         cost_estimate=pl.CostEstimate(
             flops=10**9, bytes_accessed=5 * 2**20, transcendentals=0
@@ -139,7 +148,10 @@
     out_ref[0:1, :] = weight_a
     out_ref[1:2, :] = weight_b
     out_ref[2:3, :] = seen
-    out_ref[3:8, :] = jnp.zeros((5, slots), F32)
+    out_ref[3:4, :] = weight_a + weight_b
+    out_ref[4:5, :] = jnp.where(is_a, 1.0, 0.0)
+    out_ref[5:6, :] = jnp.where(is_a, 0.0, 1.0)
+    out_ref[6:8, :] = jnp.zeros((2, slots), F32)
 
 
 def pair_weights(me, tally, value, prec, interpret=False):
@@ -172,45 +184,59 @@
 
 
 def newton_schulz(ts, eye):
-    zs = [1.5 * eye - 0.5 * t for t in ts]
-    for step in range(1, NS_ITERS):
-        cut = [split(t) for t in ts]
-        squares = [mm3(c, c) for c in cut]
-        cubes = [mm3(c, split(q)) for c, q in zip(cut, squares)]
-        ts = [2.25 * t - 1.5 * q + 0.25 * u for t, q, u in zip(ts, squares, cubes)]
-        if step < 4:
-            zs = [1.5 * z - 0.5 * mm3(split(t), split(z)) for t, z in zip(ts, zs)]
-        else:
-            zs = [z + 0.5 * mm3(split(eye - t), split(z)) for t, z in zip(ts, zs)]
-    return zs
-
-
-def centring_matrix(part):
-    r, k = iotas(264, 512)
-    ours = (k >> 2) & 1 == part
-    own = k == (r >> 2) * 8 + part * 4 + (r & 3)
-    share = jnp.where(r < 256, -1.0 / 256.0, 1.0 / 256.0)
-    return (jnp.where(ours, share, 0.0) + jnp.where(own & (r < 256), 1.0, 0.0)).astype(BF16)
+    a, b = ts
+    cut_a, cut_b = split(a), split(b)
+    z_a, z_b = 1.5 * eye - 0.5 * a, 1.5 * eye - 0.5 * b
+    square_b = mm3(cut_b, cut_b)
+    for step in range(1, NS_ITERS + 1):
+        square_a = mm3(cut_a, cut_a) if step < NS_ITERS else None
+        if step < NS_ITERS:
+            cube_b = mm3(split(square_b), cut_b)
+        if step > 1:
+            z_a = 1.5 * z_a - 0.5 * mm3(split(z_a), cut_a)
+        if step < NS_ITERS:
+            cube_a = mm3(split(square_a), cut_a)
+            b = 2.25 * b - 1.5 * square_b + 0.25 * cube_b
+            cut_b = split(b)
+            if step < NS_ITERS - 1:
+                square_b = mm3(cut_b, cut_b)
+            z_b = 1.5 * z_b - 0.5 * mm3(split(z_b), cut_b)
+            a = 2.25 * a - 1.5 * square_a + 0.25 * cube_a
+            cut_a = split(a)
+    return [z_a, z_b]
+
+
+def centring_matrix():
+    r, k = iotas(528, 128)
+    part = jnp.where(r < 512, r >> 8, r & 1)
+    own = jnp.where(r < 512, ((r & 255) >> 2) * 8 + part * 4 + (r & 3), -1)
+    share = jnp.where(
+        ((k >> 2) & 1) == part, jnp.where(r < 512, -1.0 / 256.0, 1.0 / 256.0), 0.0
+    )
+    tiles = [jnp.where(own - 128 * j == k, 255.0 / 256.0, share) for j in range(4)]
+    return jnp.concatenate(tiles, axis=1).astype(BF16)
 
 
 def analysis_kernel(recv_ref, rows_ref, out_ref, s_ref, all_ref, perturb_ref):
     slots = rows_ref.shape[1]
     half = slots // 2
-    means, middles = [], []
+    means, middles = [[], []], []
+    centre = centring_matrix()
+    for q in range(half // 256):
+        apart = mm(centre, recv_ref[:, q * 256 : (q + 1) * 256])
+        for part in range(2):
+            at = slice(part * half + q * 256, part * half + (q + 1) * 256)
+            means[part].append(apart[512 + part : 513 + part])
+            scaled = (apart[256 * part : 256 * (part + 1)] * rows_ref[3:4, at]).astype(BF16)
+            all_ref[:, at] = scaled
+            for p in range(2):
+                keep = jnp.broadcast_to(rows_ref[4 + p : 5 + p, at], (256, 256)).astype(BF16)
+                s_ref[256 * p : 256 * (p + 1), at] = scaled * keep
+    apart = mm(centre, recv_ref[:, half:])
     for part in range(2):
-        centre = centring_matrix(part)
-        for q in range(half // 256):
-            at = slice(part * half + q * 256, part * half + (q + 1) * 256)
-            apart = mm(centre, recv_ref[:, q * 256 : (q + 1) * 256])
-            means.append(apart[256:257])
-            apart = apart[:256]
-            weight_a, weight_b = rows_ref[0:1, at], rows_ref[1:2, at]
-            s_ref[0:256, at] = (apart * weight_a).astype(BF16)
-            s_ref[256:512, at] = (apart * weight_b).astype(BF16)
-            all_ref[:, at] = (apart * (weight_a + weight_b)).astype(BF16)
-        apart = mm(centre, recv_ref[:, half:])
-        middles.append(apart[256:257])
-        perturb_ref[part] = apart[:256].astype(BF16)
+        middles.append(apart[512 + part : 513 + part])
+        perturb_ref[part] = apart[256 * part : 256 * (part + 1)].astype(BF16)
+    means = means[0] + means[1]
     mean = jnp.concatenate(means, axis=1)
     weight_a, weight_b, seen = rows_ref[0:1, :], rows_ref[1:2, :], rows_ref[2:3, :]
     rest = []

time: 81.2 us -> 79.8 us (0.983)
  Pallas kernels: 14 us -> 12.5 us
    pallas_call x1, Pallas kernels: 8.1 us -> 7.03 us  [analyse(): pl.pallas_call(analysis_kernel, out_shape=jax.ShapeDtypeStruct((total, wi...]
where the time goes in v2:
time: 79.8 us; the launch traced here: 79.5 us
  waiting for transfers between devices  32.8 us (41%)
  blocking collectives  19.2 us (24%)
  starting transfers between devices  15 us (19%)
  Pallas kernels  12.5 us (16%)
    all_to_all x1, waiting for transfers between devices, exchange(): return lax.all_to_all(x, 'mem', split_axis=0, concat_axis=0, tiled=True)  32.8 us
    all_to_all x1, blocking collectives, exchange(): return lax.all_to_all(x, 'mem', split_axis=0, concat_axis=0, tiled=True)  19.2 us
    all_to_all x1, starting transfers between devices, exchange(): return lax.all_to_all(x, 'mem', split_axis=0, concat_axis=0, tiled=True)  15 us
    pallas_call x1, Pallas kernels, analyse(): pl.pallas_call(analysis_kernel, out_shape=jax.ShapeDtypeStruct((total, wi...  7.03 us
    pallas_call x1, Pallas kernels, pack(): pl.pallas_call(pack_kernel, grid=(steps,), in_specs=[pl.BlockSpec((1, pat...  3.72 us
  transfers between devices with their start and end apart: 1, of which 1 were waited for; matrix products, arithmetic and copies ran while one was open for 0% of the time, Pallas kernels for 1%

profile of v2, /device:TPU:1, one launch (start us, length us, event | category | flops | bytes accessed | tf_op | source)
XLA Modules:
  0.0 79.5 jit_solution(4575914669511282686)
XLA Ops:
  0.0 3.7 %shard_map.55 = bf16[512,1280]{1,0:T(8,128)(2,1)} custom-call(s32[1,128]{1,0:T(1,128)} %bitcast.9, bf16[4,128,2048]{2,1,0:T(8,128)(2,1)} %ens_ref.1, bf16[4,128,256]{2,1,0:T(8,128)(2,1)} %state_ref.1), custom_call_target="tpu_custom_call" | custom-call | flops 1000000000 | bytes 5242880 | tf_op jit(solution)/shard_map/pallas_call | solution.py:93
  3.7 0.0 copy-start
  3.7 0.0 copy-start.1
  3.7 0.0 copy-start.2
  3.7 15.0 %all-to-all-start = ((bf16[64,8,1280]{2,1,0:T(8,128)(2,1)}), bf16[64,8,1280]{2,1,0:T(8,128)(2,1)S(1)}, u32[]{:S(2)}, u32[]{:S(2)}) async-start(bf16[64,8,1280]{2,1,0:T(8,128)(2,1)} %bitcast.10), calls=%async_computation | async-start | bytes 2621440 | tf_op jit(solution)/shard_map/all_to_all | solution.py:310
  18.7 0.0 copy-done
  18.7 0.0 copy-done.1
  18.7 0.0 copy-done.2
  18.7 0.8 %shard_map.56.rows_ref = f32[8,2048]{1,0:T(8,128)S(1)} custom-call(s32[1]{0:T(128)} %bitcast.3.me_ref, s32[128]{0:T(128)S(1)} %copy-done.2, f32[128,2048]{1,0:T(8,128)S(1)} %copy-done, f32[128,2048]{1,0:T(8,128)S(1)} %copy-done.1), custom_call_target="tpu_custom_call" | custom-call | tf_op jit(solution)/shard_map/pallas_call | solution.py:159
  19.6 32.8 %all-to-all-done = bf16[64,8,1280]{2,1,0:T(8,128)(2,1)S(1)} async-done(((bf16[64,8,1280]{2,1,0:T(8,128)(2,1)}), bf16[64,8,1280]{2,1,0:T(8,128)(2,1)S(1)}, u32[]{:S(2)}, u32[]{:S(2)}) %all-to-all-start) | async-done | bytes 1310752 | tf_op jit(solution)/shard_map/all_to_all | solution.py:310
  52.3 7.0 %shard_map.57 = bf16[512,256]{1,0:T(8,128)(2,1)S(1)} custom-call(bf16[512,1280]{1,0:T(8,128)(2,1)S(1)} %bitcast.6, f32[8,2048]{1,0:T(8,128)S(1)} %shard_map.56.rows_ref), custom_call_target="tpu_custom_call" | custom-call | flops 5000000000 | bytes 2097152 | tf_op jit(solution)/shard_map/pallas_call | solution.py:275
  59.4 19.2 %all_to_all.22 = bf16[64,8,256]{2,1,0:T(8,128)(2,1)S(1)} all-to-all(bf16[64,8,256]{2,1,0:T(8,128)(2,1)S(1)} %bitcast.8), channel_id=1, replica_groups=mesh['mem'=64,'bal'=8] {'mem'}, dimensions={0} | all-to-all | bytes 524288 | tf_op jit(solution)/shard_map/all_to_all | solution.py:310
  78.6 0.9 %shard_map.58 = bf16[4,128,256]{2,1,0:T(8,128)(2,1)} custom-call(bf16[512,256]{1,0:T(8,128)(2,1)S(1)} %bitcast.7), custom_call_target="tpu_custom_call" | custom-call | tf_op jit(solution)/shard_map/pallas_call | solution.py:301
Async XLA Ops:
  3.7 15.0 %copy-start = (f32[128,2048]{1,0:T(8,128)S(1)}, f32[128,2048]{1,0:T(8,128)}, u32[]{:S(2)}) copy-start(f32[128,2048]{1,0:T(8,128)} %value_ref.1) | copy-start | bytes 3145732
  3.7 15.0 %copy-start.1 = (f32[128,2048]{1,0:T(8,128)S(1)}, f32[128,2048]{1,0:T(8,128)}, u32[]{:S(2)}) copy-start(f32[128,2048]{1,0:T(8,128)} %prec_ref.1) | copy-start | bytes 3145732
  3.7 15.0 %copy-start.2 = (s32[128]{0:T(128)S(1)}, s32[128]{0:T(128)}, u32[]{:S(2)}) copy-start(s32[128]{0:T(128)} %tally_ref.1) | copy-start | bytes 1540
  3.7 48.6 %all-to-all-start = ((bf16[64,8,1280]{2,1,0:T(8,128)(2,1)}), bf16[64,8,1280]{2,1,0:T(8,128)(2,1)S(1)}, u32[]{:S(2)}, u32[]{:S(2)}) async-start(bf16[64,8,1280]{2,1,0:T(8,128)(2,1)} %bitcast.10), calls=%async_computation | async-start | bytes 2621440 | tf_op jit(solution)/shard_map/all_to_all | solution.py:310

commit v3 on v2

--- a/solution.py
+++ b/solution.py
@@ -220,42 +220,47 @@
 def analysis_kernel(recv_ref, rows_ref, out_ref, s_ref, all_ref, perturb_ref):
     slots = rows_ref.shape[1]
     half = slots // 2
-    means, middles = [[], []], []
+    middles = []
     centre = centring_matrix()
+    both = None
     for q in range(half // 256):
         apart = mm(centre, recv_ref[:, q * 256 : (q + 1) * 256])
         for part in range(2):
             at = slice(part * half + q * 256, part * half + (q + 1) * 256)
-            means[part].append(apart[512 + part : 513 + part])
+            mean = apart[512 + part : 513 + part]
             scaled = (apart[256 * part : 256 * (part + 1)] * rows_ref[3:4, at]).astype(BF16)
             all_ref[:, at] = scaled
             for p in range(2):
                 keep = jnp.broadcast_to(rows_ref[4 + p : 5 + p, at], (256, 256)).astype(BF16)
                 s_ref[256 * p : 256 * (p + 1), at] = scaled * keep
+            rest = []
+            for p in range(2):
+                left = rows_ref[p : p + 1, at] * (rows_ref[2:3, at] - mean)
+                for _ in range(3):
+                    top = left.astype(BF16).astype(F32)
+                    rest.append(top)
+                    left = left - top
+            rest.append(jnp.zeros((10, 256), F32))
+            s_ref[512:528, at] = jnp.concatenate(rest, axis=0).astype(BF16)
+        if q % 2 == 2 - 1:
+            for part in range(2):
+                at = slice(part * half + (q + 1 - 2) * 256, part * half + (q + 1) * 256)
+                more = mm_nt(s_ref[:, at], all_ref[:, at])
+                both = more if both is None else both + more
     apart = mm(centre, recv_ref[:, half:])
     for part in range(2):
         middles.append(apart[512 + part : 513 + part])
         perturb_ref[part] = apart[256 * part : 256 * (part + 1)].astype(BF16)
-    means = means[0] + means[1]
-    mean = jnp.concatenate(means, axis=1)
-    weight_a, weight_b, seen = rows_ref[0:1, :], rows_ref[1:2, :], rows_ref[2:3, :]
-    rest = []
-    for w in (weight_a, weight_b):
-        left = w * (seen - mean)
-        for _ in range(3):
-            top = left.astype(BF16).astype(F32)
-            rest.append(top)
-            left = left - top
-    rest += [jnp.zeros_like(mean)] * 10
-    s_ref[512:528, :] = jnp.concatenate(rest, axis=0).astype(BF16)
-    both = mm_nt(s_ref[...], all_ref[...])
     r, c = iotas(256, 256)
     eye = jnp.where(r == c, 1.0, 0.0)
     amat = [both[256 * p : 256 * (p + 1)] + 255.0 * eye for p in range(2)]
-    fro = [jnp.sqrt(jnp.sum(a * a)) for a in amat]
+    fro = [
+        jnp.sqrt(jnp.sum(jnp.sum(a * a, axis=0, keepdims=True), axis=1, keepdims=True))
+        for a in amat
+    ]
     z = newton_schulz([a * (1.0 / f) for a, f in zip(amat, fro)], eye)
     done = []
-    for p in range(2):
+    for p in (1, 0):
         v = jnp.sum(both[512 + 3 * p : 515 + 3 * p], axis=0, keepdims=True)
         inner = jnp.sum(z[p] * v, axis=1, keepdims=True)
         mean_weights = jnp.sum(z[p] * inner, axis=0, keepdims=True) / fro[p]
@@ -264,7 +269,7 @@
     k, r = iotas(256, 256)
     scatter = one_hot(k == ((r & 127) >> 2) * 8 + (r >> 7) * 4 + (r & 3))
     for g in range(2):
-        pair = jnp.concatenate([d[128 * g : 128 * (g + 1)] for d in done], axis=0)
+        pair = jnp.concatenate([d[128 * g : 128 * (g + 1)] for d in done[::-1]], axis=0)
         out_ref[256 * g : 256 * (g + 1), :] = mm(scatter, pair).astype(BF16)
 
 

time: 79.8 us -> 79.2 us (level)
  no operation moved by 1% of the time
where the time goes in v3:
time: 79.2 us; the launch traced here: 79 us
  waiting for transfers between devices  32.8 us (41%)
  blocking collectives  19.2 us (24%)
  starting transfers between devices  15 us (19%)
  Pallas kernels  12 us (15%)
    all_to_all x1, waiting for transfers between devices, exchange(): return lax.all_to_all(x, 'mem', split_axis=0, concat_axis=0, tiled=True)  32.8 us
    all_to_all x1, blocking collectives, exchange(): return lax.all_to_all(x, 'mem', split_axis=0, concat_axis=0, tiled=True)  19.2 us
    all_to_all x1, starting transfers between devices, exchange(): return lax.all_to_all(x, 'mem', split_axis=0, concat_axis=0, tiled=True)  15 us
    pallas_call x1, Pallas kernels, analyse(): pl.pallas_call(analysis_kernel, out_shape=jax.ShapeDtypeStruct((total, wi...  6.5 us
    pallas_call x1, Pallas kernels, pack(): pl.pallas_call(pack_kernel, grid=(steps,), in_specs=[pl.BlockSpec((1, pat...  3.72 us
  transfers between devices with their start and end apart: 1, of which 1 were waited for; matrix products, arithmetic and copies ran while one was open for 0% of the time, Pallas kernels for 1%

profile of v3, /device:TPU:1, one launch (start us, length us, event | category | flops | bytes accessed | tf_op | source)
XLA Modules:
  0.0 79.0 jit_solution(4873657960234199107)
XLA Ops:
  0.0 3.7 %shard_map.55 = bf16[512,1280]{1,0:T(8,128)(2,1)} custom-call(s32[1,128]{1,0:T(1,128)} %bitcast.9, bf16[4,128,2048]{2,1,0:T(8,128)(2,1)} %ens_ref.1, bf16[4,128,256]{2,1,0:T(8,128)(2,1)} %state_ref.1), custom_call_target="tpu_custom_call" | custom-call | flops 1000000000 | bytes 5242880 | tf_op jit(solution)/shard_map/pallas_call | solution.py:93
  3.7 0.0 copy-start
  3.7 0.0 copy-start.1
  3.7 0.0 copy-start.2
  3.7 15.0 %all-to-all-start = ((bf16[64,8,1280]{2,1,0:T(8,128)(2,1)}), bf16[64,8,1280]{2,1,0:T(8,128)(2,1)S(1)}, u32[]{:S(2)}, u32[]{:S(2)}) async-start(bf16[64,8,1280]{2,1,0:T(8,128)(2,1)} %bitcast.10), calls=%async_computation | async-start | bytes 2621440 | tf_op jit(solution)/shard_map/all_to_all | solution.py:315
  18.7 0.0 copy-done
  18.7 0.0 copy-done.1
  18.7 0.0 copy-done.2
  18.7 0.8 %shard_map.56.rows_ref = f32[8,2048]{1,0:T(8,128)S(1)} custom-call(s32[1]{0:T(128)} %bitcast.3.me_ref, s32[128]{0:T(128)S(1)} %copy-done.2, f32[128,2048]{1,0:T(8,128)S(1)} %copy-done, f32[128,2048]{1,0:T(8,128)S(1)} %copy-done.1), custom_call_target="tpu_custom_call" | custom-call | tf_op jit(solution)/shard_map/pallas_call | solution.py:159
  19.6 32.8 %all-to-all-done = bf16[64,8,1280]{2,1,0:T(8,128)(2,1)S(1)} async-done(((bf16[64,8,1280]{2,1,0:T(8,128)(2,1)}), bf16[64,8,1280]{2,1,0:T(8,128)(2,1)S(1)}, u32[]{:S(2)}, u32[]{:S(2)}) %all-to-all-start) | async-done | bytes 1310752 | tf_op jit(solution)/shard_map/all_to_all | solution.py:315
  52.3 6.5 %shard_map.57 = bf16[512,256]{1,0:T(8,128)(2,1)S(1)} custom-call(bf16[512,1280]{1,0:T(8,128)(2,1)S(1)} %bitcast.6, f32[8,2048]{1,0:T(8,128)S(1)} %shard_map.56.rows_ref), custom_call_target="tpu_custom_call" | custom-call | flops 5000000000 | bytes 2097152 | tf_op jit(solution)/shard_map/pallas_call | solution.py:280
  58.9 19.2 %all_to_all.22 = bf16[64,8,256]{2,1,0:T(8,128)(2,1)S(1)} all-to-all(bf16[64,8,256]{2,1,0:T(8,128)(2,1)S(1)} %bitcast.8), channel_id=1, replica_groups=mesh['mem'=64,'bal'=8] {'mem'}, dimensions={0} | all-to-all | bytes 524288 | tf_op jit(solution)/shard_map/all_to_all | solution.py:315
  78.0 0.9 %shard_map.58 = bf16[4,128,256]{2,1,0:T(8,128)(2,1)} custom-call(bf16[512,256]{1,0:T(8,128)(2,1)S(1)} %bitcast.7), custom_call_target="tpu_custom_call" | custom-call | tf_op jit(solution)/shard_map/pallas_call | solution.py:306
Async XLA Ops:
  3.7 15.0 %copy-start = (f32[128,2048]{1,0:T(8,128)S(1)}, f32[128,2048]{1,0:T(8,128)}, u32[]{:S(2)}) copy-start(f32[128,2048]{1,0:T(8,128)} %value_ref.1) | copy-start | bytes 3145732
  3.7 15.0 %copy-start.1 = (f32[128,2048]{1,0:T(8,128)S(1)}, f32[128,2048]{1,0:T(8,128)}, u32[]{:S(2)}) copy-start(f32[128,2048]{1,0:T(8,128)} %prec_ref.1) | copy-start | bytes 3145732
  3.7 15.0 %copy-start.2 = (s32[128]{0:T(128)S(1)}, s32[128]{0:T(128)}, u32[]{:S(2)}) copy-start(s32[128]{0:T(128)} %tally_ref.1) | copy-start | bytes 1540
  3.7 48.6 %all-to-all-start = ((bf16[64,8,1280]{2,1,0:T(8,128)(2,1)}), bf16[64,8,1280]{2,1,0:T(8,128)(2,1)S(1)}, u32[]{:S(2)}, u32[]{:S(2)}) async-start(bf16[64,8,1280]{2,1,0:T(8,128)(2,1)} %bitcast.10), calls=%async_computation | async-start | bytes 2621440 | tf_op jit(solution)/shard_map/all_to_all | solution.py:315

commit v4 on v3

--- a/solution.py
+++ b/solution.py
@@ -58,12 +58,9 @@
     lower = jnp.where((r1[:, :1] >> 2) & 1 == 1, float(half), 0.0)
     _, lane = iotas(rows, 256)
     lane = lane.astype(F32)
+    firsts = []
     for g in range(groups):
         own = slice(g * patches, (g + 1) * patches)
-        there = slice(g * rows, (g + 1) * rows)
-        wanted = l1 == 2 * ((pl.program_id(0) * groups + g) * pairs + (r1 >> 3))
-        limit = jnp.sum(jnp.where(wanted, tally, 0.0), axis=1, keepdims=True) - lower
-        first = []
         for q in range(parts):
             lanes = slice(q * 256, (q + 1) * 256)
             far = slice(half + q * 256, half + (q + 1) * 256)
@@ -72,16 +69,21 @@
                 axis=0,
             )
             both = mm(take, x)
-            first.append(both[:rows])
-            second_ref[(parts - 1 - q) * rows : (parts - q) * rows, :] = both[rows:].astype(BF16)
-        turned = mm(second_ref[...], turn)
-        for q in range(parts):
-            packed_ref[there, q * 256 : (q + 1) * 256] = jnp.where(
-                lane < limit - q * 256.0, first[q], turned[q * rows : (q + 1) * rows]
-            ).astype(BF16)
+            firsts.append(both[:rows])
+            second_ref[g, (parts - 1 - q) * rows : (parts - q) * rows, :] = both[rows:].astype(BF16)
+    for g in range(groups):
+        own = slice(g * patches, (g + 1) * patches)
+        there = slice(g * rows, (g + 1) * rows)
         packed_ref[there, half:] = mm(
             take_s, state_ref[:, own, :].reshape(rows, state_ref.shape[2])
         ).astype(BF16)
+        wanted = l1 == 2 * ((pl.program_id(0) * groups + g) * pairs + (r1 >> 3))
+        limit = jnp.sum(jnp.where(wanted, tally, 0.0), axis=1, keepdims=True) - lower
+        turned = mm(second_ref[g], turn)
+        for q in range(parts):
+            packed_ref[there, q * 256 : (q + 1) * 256] = jnp.where(
+                lane < limit - q * 256.0, firsts[g * parts + q], turned[q * rows : (q + 1) * rows]
+            ).astype(BF16)
 
 
 def pack(tally, ens, state, interpret=False):
@@ -100,7 +102,7 @@
         ],
         out_specs=pl.BlockSpec((rows // steps, slots // 2 + width), lambda i: (i, 0)),
         out_shape=jax.ShapeDtypeStruct((rows, slots // 2 + width), BF16),
-        scratch_shapes=[pltpu.VMEM((512, 256), BF16)],
+        scratch_shapes=[pltpu.VMEM((2, 512, 256), BF16)],
         compiler_params=pltpu.CompilerParams(vmem_limit_bytes=PACK_VMEM),
         cost_estimate=pl.CostEstimate(
             flops=10**9, bytes_accessed=5 * 2**20, transcendentals=0

time: 79.2 us -> 79 us (level)
  no operation moved by 1% of the time
where the time goes in v4:
time: 79 us; the launch traced here: 78.7 us
  waiting for transfers between devices  32.8 us (42%)
  blocking collectives  19.2 us (24%)
  starting transfers between devices  15 us (19%)
  Pallas kernels  11.7 us (15%)
    all_to_all x1, waiting for transfers between devices, exchange(): return lax.all_to_all(x, 'mem', split_axis=0, concat_axis=0, tiled=True)  32.8 us
    all_to_all x1, blocking collectives, exchange(): return lax.all_to_all(x, 'mem', split_axis=0, concat_axis=0, tiled=True)  19.2 us
    all_to_all x1, starting transfers between devices, exchange(): return lax.all_to_all(x, 'mem', split_axis=0, concat_axis=0, tiled=True)  15 us
    pallas_call x1, Pallas kernels, analyse(): pl.pallas_call(analysis_kernel, out_shape=jax.ShapeDtypeStruct((total, wi...  6.49 us
    pallas_call x1, Pallas kernels, pack(): pl.pallas_call(pack_kernel, grid=(steps,), in_specs=[pl.BlockSpec((1, pat...  3.47 us
  transfers between devices with their start and end apart: 1, of which 1 were waited for; matrix products, arithmetic and copies ran while one was open for 0% of the time, Pallas kernels for 1%

profile of v4, /device:TPU:1, one launch (start us, length us, event | category | flops | bytes accessed | tf_op | source)
XLA Modules:
  0.0 78.7 jit_solution(12621393090446916827)
XLA Ops:
  0.0 3.5 %shard_map.55 = bf16[512,1280]{1,0:T(8,128)(2,1)} custom-call(s32[1,128]{1,0:T(1,128)} %bitcast.9, bf16[4,128,2048]{2,1,0:T(8,128)(2,1)} %ens_ref.1, bf16[4,128,256]{2,1,0:T(8,128)(2,1)} %state_ref.1), custom_call_target="tpu_custom_call" | custom-call | flops 1000000000 | bytes 5242880 | tf_op jit(solution)/shard_map/pallas_call | solution.py:95
  3.5 0.0 copy-start
  3.5 0.0 copy-start.1
  3.5 0.0 copy-start.2
  3.5 15.0 %all-to-all-start = ((bf16[64,8,1280]{2,1,0:T(8,128)(2,1)}), bf16[64,8,1280]{2,1,0:T(8,128)(2,1)S(1)}, u32[]{:S(2)}, u32[]{:S(2)}) async-start(bf16[64,8,1280]{2,1,0:T(8,128)(2,1)} %bitcast.10), calls=%async_computation | async-start | bytes 2621440 | tf_op jit(solution)/shard_map/all_to_all | solution.py:317
  18.5 0.0 copy-done
  18.5 0.0 copy-done.1
  18.5 0.0 copy-done.2
  18.5 0.8 %shard_map.56.rows_ref = f32[8,2048]{1,0:T(8,128)S(1)} custom-call(s32[1]{0:T(128)} %bitcast.3.me_ref, s32[128]{0:T(128)S(1)} %copy-done.2, f32[128,2048]{1,0:T(8,128)S(1)} %copy-done, f32[128,2048]{1,0:T(8,128)S(1)} %copy-done.1), custom_call_target="tpu_custom_call" | custom-call | tf_op jit(solution)/shard_map/pallas_call | solution.py:161
  19.3 32.8 %all-to-all-done = bf16[64,8,1280]{2,1,0:T(8,128)(2,1)S(1)} async-done(((bf16[64,8,1280]{2,1,0:T(8,128)(2,1)}), bf16[64,8,1280]{2,1,0:T(8,128)(2,1)S(1)}, u32[]{:S(2)}, u32[]{:S(2)}) %all-to-all-start) | async-done | bytes 1310752 | tf_op jit(solution)/shard_map/all_to_all | solution.py:317
  52.1 6.5 %shard_map.57 = bf16[512,256]{1,0:T(8,128)(2,1)S(1)} custom-call(bf16[512,1280]{1,0:T(8,128)(2,1)S(1)} %bitcast.6, f32[8,2048]{1,0:T(8,128)S(1)} %shard_map.56.rows_ref), custom_call_target="tpu_custom_call" | custom-call | flops 5000000000 | bytes 2097152 | tf_op jit(solution)/shard_map/pallas_call | solution.py:282
  58.6 19.2 %all_to_all.22 = bf16[64,8,256]{2,1,0:T(8,128)(2,1)S(1)} all-to-all(bf16[64,8,256]{2,1,0:T(8,128)(2,1)S(1)} %bitcast.8), channel_id=1, replica_groups=mesh['mem'=64,'bal'=8] {'mem'}, dimensions={0} | all-to-all | bytes 524288 | tf_op jit(solution)/shard_map/all_to_all | solution.py:317
  77.8 0.9 %shard_map.58 = bf16[4,128,256]{2,1,0:T(8,128)(2,1)} custom-call(bf16[512,256]{1,0:T(8,128)(2,1)S(1)} %bitcast.7), custom_call_target="tpu_custom_call" | custom-call | tf_op jit(solution)/shard_map/pallas_call | solution.py:308
Async XLA Ops:
  3.5 15.0 %copy-start = (f32[128,2048]{1,0:T(8,128)S(1)}, f32[128,2048]{1,0:T(8,128)}, u32[]{:S(2)}) copy-start(f32[128,2048]{1,0:T(8,128)} %value_ref.1) | copy-start | bytes 3145732
  3.5 15.0 %copy-start.1 = (f32[128,2048]{1,0:T(8,128)S(1)}, f32[128,2048]{1,0:T(8,128)}, u32[]{:S(2)}) copy-start(f32[128,2048]{1,0:T(8,128)} %prec_ref.1) | copy-start | bytes 3145732
  3.5 15.0 %copy-start.2 = (s32[128]{0:T(128)S(1)}, s32[128]{0:T(128)}, u32[]{:S(2)}) copy-start(s32[128]{0:T(128)} %tally_ref.1) | copy-start | bytes 1540
  3.5 48.6 %all-to-all-start = ((bf16[64,8,1280]{2,1,0:T(8,128)(2,1)}), bf16[64,8,1280]{2,1,0:T(8,128)(2,1)S(1)}, u32[]{:S(2)}, u32[]{:S(2)}) async-start(bf16[64,8,1280]{2,1,0:T(8,128)(2,1)} %bitcast.10), calls=%async_computation | async-start | bytes 2621440 | tf_op jit(solution)/shard_map/all_to_all | solution.py:317
